TPU v7x, 32 devices: a whole 2x2x4 slice. The times are simulated.
32 devices in a mesh: gx: 4 (over z), gy: 8 (over y, x, core).
Axes of the slice: x: 2, y: 2, z: 4, core: 2. Of those that a mesh axis runs over, the one named last changes fastest.
Arguments:
- particles: bfloat16 [2048, 4096], P(('gx', 'gy')), may hold values from -6 to 6
- references: bfloat16 [4, 12, 4096], P('gx'), may hold values from -1 to 1
- slot_class: int32 [4], replicated, may hold values from 0 to 3, each once
- log_prior: float32 [4], replicated, may hold values from -2 to 2
- shift_offsets: int32 [8, 2], replicated, may hold values from -8 to 8
- group_ids: int32 [2048], P(('gx', 'gy')), may hold values from 0 to 127
- ctf_table: float32 [128, 2048], replicated, may hold values from -1 to 1
- noise_power: float32 [2048], replicated, may hold values from 0.5 to 2
Outputs:
- class_sums: float32 [4, 12, 4096], P('gx')
- ctf_power: float32 [4, 2048], P('gx')
- log_evidence: float32 [], replicated
Inputs may be any that keep to these rules, and one draw needn't show every extreme that they name: `slot_class`: each class id stands at exactly one slot.
All inputs are finite; a program needn't handle non-finite values.
Results may differ from a plain program's by a relative error of at most 0.006.
Values may be sent and summed in bfloat16 or wider, within the bound.
No kernel may reach another device: no remote copies, remote signals or barrier semaphores. Data moves between devices by JAX's collectives and lax.ppermute only.
A program may use at most 64 MiB of HBM per device.

v0:
```python
import jax
import jax.numpy as jnp
from jax import lax
from jax.sharding import PartitionSpec as P

L = 64
R = 12
NS = 8
G = 128
HALF = 2048
FR = 4096


def phase_tables(shift_offsets, edge_len):
    half_size = edge_len * edge_len // 2
    freq_index = jnp.arange(half_size, dtype=jnp.int32)
    row_freq = freq_index // (edge_len // 2)
    col_freq = freq_index % (edge_len // 2)
    phase_turns = jnp.mod(
        row_freq[None, :] * shift_offsets[:, 0:1] + col_freq[None, :] * shift_offsets[:, 1:2],
        edge_len,
    )
    angles = phase_turns.astype(jnp.float32) * (2.0 * jnp.pi / edge_len)
    return (jnp.cos(angles), jnp.sin(angles))


def spectra(particles, edge_len):
    rows_here = particles.shape[0]
    half_side = edge_len // 2
    images = particles.astype(jnp.float32).reshape(rows_here * edge_len, edge_len)
    pixel_index = jnp.arange(edge_len, dtype=jnp.int32)
    column_turns = jnp.mod(pixel_index[:, None] * pixel_index[None, :half_side], edge_len).astype(
        jnp.float32
    ) * (2.0 * jnp.pi / edge_len)
    column_table = jnp.concatenate([jnp.cos(column_turns), -jnp.sin(column_turns)], axis=1)
    partial_x = jnp.dot(
        images, column_table, precision=lax.Precision.HIGHEST, preferred_element_type=jnp.float32
    )
    partial_x = partial_x.reshape(rows_here, edge_len, edge_len)
    row_turns = jnp.mod(pixel_index[:, None] * pixel_index[None, :], edge_len).astype(
        jnp.float32
    ) * (2.0 * jnp.pi / edge_len)
    with_cos = jnp.einsum(
        "uy,pyw->puw", jnp.cos(row_turns), partial_x, precision=lax.Precision.HIGHEST
    )
    with_sin = jnp.einsum(
        "uy,pyw->puw", jnp.sin(row_turns), partial_x, precision=lax.Precision.HIGHEST
    )
    real_part = (with_cos[..., :half_side] + with_sin[..., half_side:]) / edge_len
    imag_part = (with_cos[..., half_side:] - with_sin[..., :half_side]) / edge_len
    return (real_part.reshape(rows_here, -1), imag_part.reshape(rows_here, -1))


def shards(
    particles, references, slot_class, log_prior, shift_offsets, group_ids, ctf_table, noise_power
):
    rows_here = particles.shape[0]
    classes = lax.axis_size("gx") * references.shape[0]
    row_width = R * NS
    real_part, imag_part = spectra(particles, L)
    inv_noise = 1.0 / noise_power
    group_hot = (group_ids[:, None] == jnp.arange(G, dtype=jnp.int32)[None, :]).astype(jnp.float32)
    ctf_rows = jnp.dot(
        group_hot, ctf_table, precision=lax.Precision.HIGHEST, preferred_element_type=jnp.float32
    )
    whiten = ctf_rows * inv_noise
    weighted = jnp.concatenate([real_part * whiten, imag_part * whiten], axis=1).astype(
        jnp.bfloat16
    )
    data_power = jnp.sum((real_part * real_part + imag_part * imag_part) * inv_noise, axis=1)
    cosines, sine_table = phase_tables(shift_offsets, L)
    power_table = ctf_table * ctf_table * inv_noise
    blank = jnp.zeros((rows_here, classes * row_width), jnp.float32)
    piece = lax.all_gather(references, "gx", axis=0, tiled=True)

    def add_class(offset, table):
        stack_row = lax.dynamic_index_in_dim(piece, offset, 0, keepdims=False).astype(jnp.float32)
        stack_real = stack_row[:, :HALF]
        stack_imag = stack_row[:, HALF:]
        shifted_real = (
            stack_real[:, None, :] * cosines[None] + stack_imag[:, None, :] * sine_table[None]
        )
        shifted_imag = (
            stack_imag[:, None, :] * cosines[None] - stack_real[:, None, :] * sine_table[None]
        )
        shifted = (
            jnp.concatenate([shifted_real, shifted_imag], axis=2)
            .astype(jnp.bfloat16)
            .reshape(row_width, FR)
        )
        intersection = lax.dot_general(
            weighted, shifted, (((1,), (1,)), ((), ())), preferred_element_type=jnp.float32
        )
        amplitude = stack_real * stack_real + stack_imag * stack_imag
        ref_power = jnp.dot(
            power_table,
            amplitude.T,
            precision=lax.Precision.HIGHEST,
            preferred_element_type=jnp.float32,
        )
        own_power = jnp.dot(
            group_hot,
            ref_power,
            precision=lax.Precision.HIGHEST,
            preferred_element_type=jnp.float32,
        )
        logits = intersection.reshape(rows_here, R, NS) - 0.5 * own_power[:, :, None]
        return lax.dynamic_update_slice_in_dim(
            table, logits.reshape(rows_here, row_width), offset * row_width, 1
        )

    scores = lax.fori_loop(0, piece.shape[0], add_class, blank)
    slot_prior = jnp.sum(
        jnp.where(
            slot_class[:, None] == jnp.arange(classes, dtype=jnp.int32)[None, :],
            log_prior[None, :],
            0.0,
        ),
        axis=1,
    )
    logits = (
        scores.reshape(rows_here, classes, row_width)
        - 0.5 * data_power[:, None, None]
        + slot_prior[None, :, None]
    )
    row_max = jnp.max(logits, axis=(1, 2), keepdims=True)
    raised = jnp.exp(logits - row_max)
    normaliser = jnp.sum(raised, axis=(1, 2), keepdims=True)
    weights = raised / normaliser
    evidence = row_max[:, 0, 0] + jnp.log(normaliser[:, 0, 0])
    weights_low = weights.astype(jnp.bfloat16)
    group_weights = jnp.dot(
        jnp.sum(weights, axis=2).T,
        group_hot,
        precision=lax.Precision.HIGHEST,
        preferred_element_type=jnp.float32,
    )

    def class_terms(slot_index):
        weight_cols = lax.dynamic_index_in_dim(weights_low, slot_index, 1, keepdims=False)
        moment = lax.dot_general(
            weight_cols, weighted, (((0,), (0,)), ((), ())), preferred_element_type=jnp.float32
        )
        moment = moment.reshape(R, NS, FR)
        moment_real = moment[..., :HALF]
        moment_imag = moment[..., HALF:]
        back_real = jnp.sum(moment_real * cosines[None] - moment_imag * sine_table[None], axis=1)
        back_imag = jnp.sum(moment_imag * cosines[None] + moment_real * sine_table[None], axis=1)
        return jnp.concatenate([back_real, back_imag], axis=1)

    owned = lax.psum_scatter(
        lax.map(
            lambda offset: class_terms(offset),
            jnp.arange(references.shape[0] * lax.axis_size("gx"), dtype=jnp.int32),
        ),
        "gx",
        scatter_dimension=0,
        tiled=True,
    )
    class_sums = lax.psum(owned, "gy")
    totals, evidence_sum = lax.psum((group_weights, jnp.sum(evidence)), ("gx", "gy"))
    own_groups = lax.dynamic_slice_in_dim(totals, lax.axis_index("gx"), 1, 0)
    ctf_power = jnp.dot(
        own_groups,
        ctf_table * ctf_table,
        precision=lax.Precision.HIGHEST,
        preferred_element_type=jnp.float32,
    )
    log_evidence = evidence_sum / (rows_here * lax.axis_size("gx") * lax.axis_size("gy") * HALF)
    return (class_sums, ctf_power, log_evidence)


def solution(mesh):
    return jax.shard_map(
        shards,
        mesh=mesh,
        in_specs=(
            P(("gx", "gy"), None),
            P("gx", None, None),
            P(),
            P(),
            P(),
            P(("gx", "gy")),
            P(),
            P(),
        ),
        out_specs=(P("gx", None, None), P("gx", None), P()),
        check_vma=False,
    )
```

profile of v0, /device:TPU:0, one launch (start us, length us, event | category | flops | bytes accessed | tf_op | source)
XLA Modules:
  0.0 206.5 jit_solution(13460478304987082292)
XLA Ops:
  7.4 2.1 reshape.111
  9.4 1.3 convolution_bitcast_fusion.1
  11.6 4.6 %fusion.46 = f32[64,64,64]{1,2,0:T(8,128)} fusion(f32[64,64,64]{1,0,2:T(8,128)S(1)} %reshape.112), kind=kOutput, calls=%fused_computation.59 | convolution fusion | flops 201383936 | bytes 2097152 | tf_op jit(solution)/shard_map/uy,pyw->puw/dot_general | solution.py:43
  16.2 4.7 %fusion.49 = f32[64,64,64]{1,2,0:T(8,128)} fusion(f32[64,64,64]{1,0,2:T(8,128)S(1)} %reshape.112), kind=kOutput, calls=%fused_computation.60 | convolution fusion | flops 201383936 | bytes 2097152 | tf_op jit(solution)/shard_map/uy,pyw->puw/dot_general | solution.py:46
  21.7 3.4 %multiply_reduce_fusion = (f32[64]{0:T(128)}, f32[64,64,32]{1,2,0:T(8,128)S(1)}, f32[64,64,32]{1,2,0:T(8,128)S(1)}) fusion(f32[64,32]{0,1:T(8,128)S(1)} %copy.44, f32[64,64,64]{1,2,0:T(8,128)} %fusion.49, f32[64,64,64]{1,2,0:T(8,128)} %fusion.46), kind=kLoop, calls=%fused_computation.65 | loop fusion | flops 1179584 | bytes 3154176 | tf_op jit(solution)/shard_map/reduce_sum | solution.py:70
  25.1 1.1 copy.39
  26.1 1.1 copy.40
  27.3 1.1 copy.41
  28.4 1.1 copy.42
  30.3 18.2 %all_gather.3 = bf16[4,12,4096]{2,1,0:T(8,128)(2,1)} all-gather(bf16[1,12,4096]{2,1,0:T(8,128)(2,1)S(1)} %copy-done.3), channel_id=1, replica_groups=mesh['gx'=4,'gy'=8] {'gx'}, dimensions={0}, use_global_device_ids=true | all-gather | bytes 491520 | tf_op jit(solution)/shard_map/all_gather | solution.py:74
  48.4 1.2 multiply_convert_fusion.1
  49.7 25.9 %while.27 = (s32[]{:T(128)}, f32[64,384]{1,0:T(8,128)S(1)}, bf16[4,12,4096]{2,1,0:T(8,128)(2,1)}, bf16[64,4096]{1,0:T(8,128)(2,1)S(1)}, f32[128,2048]{1,0:T(8,12...) while((s32[]{:T(128)}, f32[64,384]{1,0:T(8,128)S(1)}, ...), condition=%wide.region_1.2_spmd.clone.clone, body=%wide.region_0.1_spmd.clone.clone.sunk | while | flops 92814080 | bytes 4696571 | solution.py:112
  50.7 1.1 fusion.137
  54.5 1.2 fusion.140
  57.1 1.1 fusion.137
  60.9 1.2 fusion.140
  63.6 1.1 fusion.137
  67.4 1.2 fusion.140
  74.0 1.2 fusion.140
  78.0 21.0 %while.28 = (s32[]{:T(128)}, f32[4,12,4096]{2,1,0:T(8,128)}, s32[4]{0:T(128)S(1)}, bf16[64,4,96]{0,2,1:T(8,128)(2,1)S(1)}, bf16[64,4096]{1,0:T(8,128)(2,1)S(1)},...) while((s32[]{:T(128)}, f32[4,12,4096]{2,1,0:T(8,128)}, ...), condition=%wide.region_9.10_spmd.clone.clone, body=%wide.region_6.9_spmd.clone.clone.sunk | while | flops 52166660 | bytes 4629223 | solution.py:152
  100.5 42.4 %all-reduce = (f32[4,128]{1,0:T(4,128)S(1)}, f32[]{:T(128)}) all-reduce(f32[4,128]{1,0:T(4,128)S(1)} %fusion.68, f32[]{:T(128)} %add_reduce_fusion.1), channel_id=1, replica_groups=mesh['gx'=4,'gy'=8] {'gx','gy'}, use_global_device_ids=true, to_apply=%region_13.14 | all-reduce | flops 513 | bytes 4104 | tf_op jit(solution)/shard_map/psum | solution.py:161
  143.0 1.2 fusion.54
  144.9 51.8 %all-reduce.3.cloned.1.call-done = f32[1,12,4096]{2,1,0:T(8,128)} async-done(((f32[1,12,4096]{2,1,0:T(8,128)}), f32[1,12,4096]{2,1,0:T(8,128)}) %all-reduce.3.cloned.1.call-update) | async-done | bytes 196624 | tf_op jit(solution)/shard_map/psum | solution.py:160
  196.7 1.8 copy.45
  (93 shorter events, 37.4 us)
Async XLA Ops:
  7.2 135.8 %reduce-scatter.2.cloned.1.call-start = ((), (), s32[]{:S(2)}) async-start(), calls=%async_computation.1 | async-start | bytes 1310720 | tf_op jit(solution)/shard_map/reduce_scatter | solution.py:151
  16.2 5.3 %copy-start.4 = (f32[2048]{0:T(1024)S(1)}, f32[2048]{0:T(1024)}, u32[]{:S(2)}) copy-start(f32[2048]{0:T(1024)} %param.19) | copy-start | bytes 24580
  27.3 2.3 %copy-start = (f32[128,2048]{1,0:T(8,128)S(1)}, f32[128,2048]{1,0:T(8,128)}, u32[]{:S(2)}) copy-start(f32[128,2048]{1,0:T(8,128)} %param.18) | copy-start | bytes 3145732
  28.4 1.3 copy-start.5
  28.4 1.9 copy-start.3
  29.5 18.9 %copy-start.1 = (f32[64,2048]{1,0:T(8,128)S(1)}, f32[64,2048]{1,0:T(8,128)}, u32[]{:S(2)}) copy-start(f32[64,2048]{1,0:T(8,128)} %copy.40) | copy-start | bytes 1572868
  29.5 18.9 %copy-start.2 = (f32[64,2048]{1,0:T(8,128)S(1)}, f32[64,2048]{1,0:T(8,128)}, u32[]{:S(2)}) copy-start(f32[64,2048]{1,0:T(8,128)} %copy.42) | copy-start | bytes 1572868
  99.0 97.7 %all-reduce.3.cloned.1.call-start = ((), (), s32[]{:S(2)}) async-start(), calls=%async_computation.2 | async-start | bytes 524288 | tf_op jit(solution)/shard_map/psum | solution.py:160
Sparse Core Ops, SparseCore 0:
  99.2 29.8 reduce-scatter.1
  143.1 53.5 all-reduce.2
where the time goes:
time: 208 us; the launch traced here: 206 us
  blocking collectives  60.6 us (29%)
  waiting for transfers between devices  51.9 us (25%)
  matrix products  27.2 us (13%)
  other arithmetic  25.1 us (12%)
  local copies, waits for them, and re-layouts  17.6 us (8%)
  between operations  16 us (8%)
  loops' own time  8.13 us (4%)
    psum x1, waiting for transfers between devices, shards(): class_sums = lax.psum(owned, 'gy')  51.8 us
    psum x1, blocking collectives, shards(): lax.psum((group_weights, jnp.sum(evidence)), ('gx', 'gy'))  42.4 us
    all_gather x1, blocking collectives, shards(): piece = lax.all_gather(references, 'gx', axis=0, tiled=True)  18.2 us
    cos x8, other arithmetic, phase_tables(): return (jnp.cos(angles), jnp.sin(angles))  8.53 us
    another operation x1, loops' own time, shards(): lax.map(lambda offset: class_terms(offset), jnp.arange(references.shape[0...  7.85 us
    dot_general x1, matrix products, spectra(): jnp.einsum('uy,pyw->puw', jnp.sin(row_turns), partial_x, precision=lax.Pr...  4.7 us
    dot_general x1, matrix products, spectra(): jnp.einsum('uy,pyw->puw', jnp.cos(row_turns), partial_x, precision=lax.Pr...  4.65 us
    dot_general x4, matrix products, add_class(): lax.dot_general(weighted, shifted, (((1,), (1,)), ((), ())), preferred_el...  4.62 us
  transfers between devices with their start and end apart: 2, of which 1 were waited for; matrix products, arithmetic and copies ran while one was open for 1% of the time, Pallas kernels for 0%

commit v1 on v0

--- a/solution.py
+++ b/solution.py
@@ -71,7 +71,16 @@
     cosines, sine_table = phase_tables(shift_offsets, L)
     power_table = ctf_table * ctf_table * inv_noise
     blank = jnp.zeros((rows_here, classes * row_width), jnp.float32)
-    piece = lax.all_gather(references, "gx", axis=0, tiled=True)
+    ways = lax.axis_size("gx")
+    up = [(d, (d + 1) % ways) for d in range(ways)]
+    down = [(d, (d - 1) % ways) for d in range(ways)]
+    earlier, later = ([references], [references])
+    for _ in range(ways // 2):
+        earlier.append(lax.ppermute(earlier[-1], "gx", up))
+    for _ in range((ways - 1) // 2):
+        later.append(lax.ppermute(later[-1], "gx", down))
+    line = jnp.concatenate([*earlier[::-1], *later[1:]], axis=0)
+    piece = jnp.roll(line, (lax.axis_index("gx") - ways // 2) * references.shape[0], axis=0)
 
     def add_class(offset, table):
         stack_row = lax.dynamic_index_in_dim(piece, offset, 0, keepdims=False).astype(jnp.float32)

time: 208 us -> 201 us (0.966)
  blocking collectives: 60.6 us -> 39.2 us
  waiting for transfers between devices: 51.9 us -> 58.5 us
  starting transfers between devices: 0.08 us -> 5.28 us
    all_gather x1 -> x0, blocking collectives: 18.2 us -> none  [shards(): piece = lax.all_gather(references, 'gx', axis=0, tiled=True)]
    ppermute x0 -> x3, waiting for transfers between devices: none -> 6.16 us  [the longest x2 6.16 us: shards(): earlier.append(lax.ppermute(earlier[-1], 'gx', up))]
    ppermute x0 -> x3, starting transfers between devices: none -> 5.2 us  [the longest x2 3.11 us: shards(): earlier.append(lax.ppermute(earlier[-1], 'gx', up))]
    psum x1, blocking collectives: 42.4 us -> 39.2 us  [shards(): lax.psum((group_weights, jnp.sum(evidence)), ('gx', 'gy'))]
  transfers between devices with their start and end apart: 2 -> 5, of which waited for: 1 -> 2; matrix products, arithmetic and copies ran while one was open for 1% -> 14% of each run, Pallas kernels for 0% -> 0%
where the time goes in v1:
time: 201 us; the launch traced here: 199 us
  waiting for transfers between devices  58.5 us (29%)
  blocking collectives  39.2 us (20%)
  matrix products  27.4 us (14%)
  other arithmetic  25.7 us (13%)
  local copies, waits for them, and re-layouts  19.1 us (10%)
  between operations  16.1 us (8%)
  loops' own time  8.12 us (4%)
  starting transfers between devices  5.28 us (3%)
    psum x1, waiting for transfers between devices, shards(): class_sums = lax.psum(owned, 'gy')  52.3 us
    psum x1, blocking collectives, shards(): lax.psum((group_weights, jnp.sum(evidence)), ('gx', 'gy'))  39.2 us
    cos x8, other arithmetic, phase_tables(): return (jnp.cos(angles), jnp.sin(angles))  8.53 us
    another operation x1, loops' own time, shards(): lax.map(lambda offset: class_terms(offset), jnp.arange(references.shape[0...  7.85 us
    ppermute x2, waiting for transfers between devices, shards(): earlier.append(lax.ppermute(earlier[-1], 'gx', up))  6.16 us
    dot_general x1, matrix products, spectra(): jnp.einsum('uy,pyw->puw', jnp.sin(row_turns), partial_x, precision=lax.Pr...  4.7 us
    dot_general x1, matrix products, spectra(): jnp.einsum('uy,pyw->puw', jnp.cos(row_turns), partial_x, precision=lax.Pr...  4.65 us
    dot_general x4, matrix products, add_class(): lax.dot_general(weighted, shifted, (((1,), (1,)), ((), ())), preferred_el...  4.62 us
  transfers between devices with their start and end apart: 5, of which 2 were waited for; matrix products, arithmetic and copies ran while one was open for 14% of the time, Pallas kernels for 0%

profile of v1, /device:TPU:0, one launch (start us, length us, event | category | flops | bytes accessed | tf_op | source)
XLA Modules:
  0.0 199.4 jit_solution(4063208097756381915)
XLA Ops:
  7.2 3.1 %collective-permute-start = (bf16[1,12,4096]{2,1,0:T(8,128)(2,1)}, bf16[1,12,4096]{2,1,0:T(8,128)(2,1)S(1)}, u32[]{:S(2)}, u32[]{:S(2)}) collective-permute-start(bf16[1,12,4096]{2,1,0:T(8,128)(2,1)} %param.13), channel_id=1, source_target_pairs={{0,8},{8,16},{16,24},{24,0},{1,9},{9,17},{17,25},{25,1},{2,10},{10... | collective-permute-start | bytes 294920 | tf_op jit(solution)/shard_map/ppermute | solution.py:79
  10.3 2.1 %collective-permute-start.2 = (bf16[1,12,4096]{2,1,0:T(8,128)(2,1)}, bf16[1,12,4096]{2,1,0:T(8,128)(2,1)S(1)}, u32[]{:S(2)}, u32[]{:S(2)}) collective-permute-start(bf16[1,12,4096]{2,1,0:T(8,128)(2,1)} %param.13), channel_id=1, source_target_pairs={{0,24},{8,0},{16,8},{24,16},{1,25},{9,1},{17,9},{25,17},{2,26},{10... | collective-permute-start | bytes 294920 | tf_op jit(solution)/shard_map/ppermute | solution.py:81
  12.6 2.1 %reshape.111 = bf16[4096,64]{1,0:T(8,128)(2,1)S(1)} reshape(bf16[64,4096]{1,0:T(8,128)(2,1)} %param.12) | data formatting | bytes 1048576 | tf_op jit(solution)/shard_map/reshape | solution.py:30
  14.6 1.3 convolution_bitcast_fusion.1
  16.8 4.6 %fusion.46 = f32[64,64,64]{1,2,0:T(8,128)} fusion(f32[64,64,64]{1,0,2:T(8,128)S(1)} %reshape.112), kind=kOutput, calls=%fused_computation.59 | convolution fusion | flops 201383936 | bytes 2097152 | tf_op jit(solution)/shard_map/uy,pyw->puw/dot_general | solution.py:43
  21.4 4.7 %fusion.49 = f32[64,64,64]{1,2,0:T(8,128)} fusion(f32[64,64,64]{1,0,2:T(8,128)S(1)} %reshape.112), kind=kOutput, calls=%fused_computation.60 | convolution fusion | flops 201383936 | bytes 2097152 | tf_op jit(solution)/shard_map/uy,pyw->puw/dot_general | solution.py:46
  26.3 2.8 %multiply_reduce_fusion = (f32[64]{0:T(128)S(1)}, f32[64,64,32]{1,2,0:T(8,128)S(1)}, f32[64,64,32]{1,2,0:T(8,128)S(1)}) fusion(f32[64,32]{0,1:T(8,128)S(1)} %copy.44, f32[64,64,64]{1,2,0:T(8,128)} %fusion.49, f32[64,64,64]{1,2,0:T(8,128)} %fusion.46), kind=kLoop, calls=%fused_computation.65 | loop fusion | flops 1179584 | bytes 3154176 | tf_op jit(solution)/shard_map/reduce_sum | solution.py:70
  29.1 1.1 copy.39
  30.2 1.1 copy.40
  31.3 1.1 copy.41
  32.4 1.1 copy.42
  34.8 1.4 multiply_convert_fusion.1
  37.9 6.2 %collective-permute-done.1 = bf16[1,12,4096]{2,1,0:T(8,128)(2,1)S(1)} collective-permute-done((bf16[1,12,4096]{2,1,0:T(8,128)(2,1)S(1)}, bf16[1,12,4096]{2,1,0:T(8,128)(2,1)S(1)}, u32[]{:S(2)}, u32[]{:S(2)}) %collective-permute-start.1) | collective-permute-done | bytes 98336 | tf_op jit(solution)/shard_map/ppermute | solution.py:79
  45.0 25.9 %while.27 = (s32[]{:T(128)}, f32[64,384]{1,0:T(8,128)S(1)}, bf16[4,12,4096]{2,1,0:T(8,128)(2,1)}, bf16[64,4096]{1,0:T(8,128)(2,1)S(1)}, f32[128,2048]{1,0:T(8,12...) while((s32[]{:T(128)}, f32[64,384]{1,0:T(8,128)S(1)}, ...), condition=%wide.region_1.2_spmd.clone.clone, body=%wide.region_0.1_spmd.clone.clone.sunk | while | flops 92814080 | bytes 4696571 | solution.py:121
  46.0 1.1 fusion.137
  49.8 1.2 fusion.140
  56.2 1.2 fusion.140
  62.8 1.2 fusion.140
  69.3 1.2 fusion.140
  73.7 21.0 %while.28 = (s32[]{:T(128)}, f32[4,12,4096]{2,1,0:T(8,128)}, s32[4]{0:T(128)S(1)}, bf16[64,4,96]{0,2,1:T(8,128)(2,1)S(1)}, bf16[64,4096]{1,0:T(8,128)(2,1)S(1)},...) while((s32[]{:T(128)}, f32[4,12,4096]{2,1,0:T(8,128)}, ...), condition=%wide.region_9.10_spmd.clone.clone, body=%wide.region_6.9_spmd.clone.clone.sunk | while | flops 52166660 | bytes 4629223 | solution.py:161
  96.2 39.2 %all-reduce = (f32[4,128]{1,0:T(4,128)S(1)}, f32[]{:T(128)}) all-reduce(f32[4,128]{1,0:T(4,128)S(1)} %fusion.68, f32[]{:T(128)} %add_reduce_fusion.1), channel_id=1, replica_groups=mesh['gx'=4,'gy'=8] {'gx','gy'}, use_global_device_ids=true, to_apply=%region_13.14 | all-reduce | flops 513 | bytes 4104 | tf_op jit(solution)/shard_map/psum | solution.py:170
  135.4 1.2 fusion.54
  137.3 52.3 %all-reduce.3.cloned.1.call-done = f32[1,12,4096]{2,1,0:T(8,128)} async-done(((f32[1,12,4096]{2,1,0:T(8,128)}), f32[1,12,4096]{2,1,0:T(8,128)}) %all-reduce.3.cloned.1.call-update) | async-done | bytes 196624 | tf_op jit(solution)/shard_map/psum | solution.py:169
  189.6 1.8 copy.45
  (113 shorter events, 42.3 us)
Async XLA Ops:
  7.2 128.2 %reduce-scatter.2.cloned.1.call-start = ((), (), s32[]{:S(2)}) async-start(), calls=%async_computation.1 | async-start | bytes 1310720 | tf_op jit(solution)/shard_map/reduce_scatter | solution.py:160
  7.2 30.1 %collective-permute-start = (bf16[1,12,4096]{2,1,0:T(8,128)(2,1)}, bf16[1,12,4096]{2,1,0:T(8,128)(2,1)S(1)}, u32[]{:S(2)}, u32[]{:S(2)}) collective-permute-start(bf16[1,12,4096]{2,1,0:T(8,128)(2,1)} %param.13), channel_id=1, source_target_pairs={{0,8},{8,16},{16,24},{24,0},{1,9},{9,17},{17,25},{25,1},{2,10},{10... | collective-permute-start | bytes 294920 | tf_op jit(solution)/shard_map/ppermute | solution.py:79
  10.3 33.8 %collective-permute-start.2 = (bf16[1,12,4096]{2,1,0:T(8,128)(2,1)}, bf16[1,12,4096]{2,1,0:T(8,128)(2,1)S(1)}, u32[]{:S(2)}, u32[]{:S(2)}) collective-permute-start(bf16[1,12,4096]{2,1,0:T(8,128)(2,1)} %param.13), channel_id=1, source_target_pairs={{0,24},{8,0},{16,8},{24,16},{1,25},{9,1},{17,9},{25,17},{2,26},{10... | collective-permute-start | bytes 294920 | tf_op jit(solution)/shard_map/ppermute | solution.py:81
  21.4 4.7 %copy-start.4 = (f32[2048]{0:T(1024)S(1)}, f32[2048]{0:T(1024)}, u32[]{:S(2)}) copy-start(f32[2048]{0:T(1024)} %param.19) | copy-start | bytes 24580
  31.3 2.2 %copy-start = (f32[128,2048]{1,0:T(8,128)S(1)}, f32[128,2048]{1,0:T(8,128)}, u32[]{:S(2)}) copy-start(f32[128,2048]{1,0:T(8,128)} %param.18) | copy-start | bytes 3145732
  32.4 1.3 copy-start.6
  32.4 2.4 %copy-start.1 = (f32[64,2048]{1,0:T(8,128)S(1)}, f32[64,2048]{1,0:T(8,128)}, u32[]{:S(2)}) copy-start(f32[64,2048]{1,0:T(8,128)} %copy.40) | copy-start | bytes 1572868
  33.5 1.3 copy-start.2
  33.6 2.7 %copy-start.7 = (f32[4]{0:T(128)S(1)}, f32[4]{0:T(128)}, u32[]{:S(2)}) copy-start(f32[4]{0:T(128)} %param.15) | copy-start | bytes 52
  33.7 2.7 %copy-start.8 = (s32[4]{0:T(128)S(1)}, s32[4]{0:T(128)}, u32[]{:S(2)}) copy-start(s32[4]{0:T(128)} %param.14) | copy-start | bytes 52
  34.8 9.2 %copy-start.3 = (bf16[1,12,4096]{2,1,0:T(8,128)(2,1)S(1)}, bf16[1,12,4096]{2,1,0:T(8,128)(2,1)}, u32[]{:S(2)}) copy-start(bf16[1,12,4096]{2,1,0:T(8,128)(2,1)} %param.13) | copy-start | bytes 294916
  36.5 0.7 copy-start.5
  37.3 6.8 %collective-permute-start.1 = (bf16[1,12,4096]{2,1,0:T(8,128)(2,1)S(1)}, bf16[1,12,4096]{2,1,0:T(8,128)(2,1)S(1)}, u32[]{:S(2)}, u32[]{:S(2)}) collective-permute-start(bf16[1,12,4096]{2,1,0:T(8,128)(2,1)S(1)} %collective-permute-done), channel_id=1, source_target_pairs={{0,8},{8,16},{16,24},{24,0},{1,9},{9,17},{17,25},{25,1},{2,10},{10... | collective-permute-start | bytes 294920 | tf_op jit(solution)/shard_map/ppermute | solution.py:79
  94.7 94.9 %all-reduce.3.cloned.1.call-start = ((), (), s32[]{:S(2)}) async-start(), calls=%async_computation.2 | async-start | bytes 524288 | tf_op jit(solution)/shard_map/psum | solution.py:169
Sparse Core Ops, SparseCore 0:
  94.8 26.3 reduce-scatter.1
  135.6 53.9 all-reduce.2
